TPU v7x, 32 devices: a whole 2x2x4 slice. The times are simulated.
32 devices in a mesh: patch: 8 (over z, x), sub: 4 (over y, core).
Axes of the slice: x: 2, y: 2, z: 4, core: 2. Of those that a mesh axis runs over, the one named last changes fastest.
Arguments:
- displacement: float32 [3, 64, 8192], P(None, 'patch', 'sub'), may hold values from -3 to 3
- load: float32 [3, 64, 8192], P(None, 'patch', 'sub'), may hold values from -6 to 6
- foundation: float32 [3, 64, 8192], P(None, 'patch', 'sub'), may hold values from 0.2 to 2
- layup: int32 [64, 8192], P('patch', 'sub'), may hold values from 0 to 7
- layup_stiffness: float32 [8, 6, 6], replicated, as said below
- w_first: bfloat16 [128, 6], replicated, may hold values from -2.5 to 2.5
- w_mid: bfloat16 [3, 128, 128], replicated, may hold values from -0.5 to 0.5
- w_last: bfloat16 [6, 128], replicated, may hold values from -0.5 to 0.5
Outputs:
- residual: float32 [3, 64, 8192], P(None, 'patch', 'sub')
- adjoint: float32 [3, 64, 8192], P(None, 'patch', 'sub')
- grad_first: float32 [128, 6], replicated
- grad_mid: float32 [3, 128, 128], replicated
- grad_last: float32 [6, 128], replicated
Inputs may be any that keep to these rules, and one draw needn't show every extreme that they name: `layup_stiffness`: each of the 8 matrices is symmetric positive definite.
All inputs are finite; a program needn't handle non-finite values.
Results may differ from a plain program's by a relative error of at most 0.0006.
The roundings to bfloat16 on the way count: a program that leaves them out, or rounds other values in their place, can miss the bound.
Values sent between devices are 32-bit elements; how exact they have to be, the bound alone decides.
No kernel may reach another device: no remote copies, remote signals or barrier semaphores. Data moves between devices by JAX's collectives and lax.ppermute only.
A program may use at most 128 MiB of HBM per device.

v0:
```python
import jax
import jax.numpy as jnp
from jax import lax
from jax.sharding import PartitionSpec as P

ITERS = 4
BASIS_VALUE = (0.125, 0.75, 0.125)
BASIS_SLOPE = (-0.5, 0.0, 0.5)
BASIS_CURVE = (1.0, -2.0, 1.0)
HOOP_CURVATURE = 0.25


def padded_2(cells, sides, width):
    for axis, dim in sides:
        count = lax.axis_size(axis)
        head = lax.slice_in_dim(cells, 0, width, axis=dim)
        tail = lax.slice_in_dim(cells, cells.shape[dim] - width, cells.shape[dim], axis=dim)
        cells = jnp.concatenate(
            [
                lax.ppermute(tail, axis, [(i, (i + 1) % count) for i in range(count)]),
                cells,
                lax.ppermute(head, axis, [((i + 1) % count, i) for i in range(count)]),
            ],
            axis=dim,
        )
    return cells


def correlate(padded, along_x, along_y):
    row_count = padded.shape[-2] - 2
    col_count = padded.shape[-1] - 2
    partial_x = None
    for offset in range(3):
        if along_x[offset] != 0.0:
            weighted = along_x[offset] * padded[..., offset : offset + row_count, :]
            partial_x = weighted if partial_x is None else partial_x + weighted
    running = None
    for offset in range(3):
        if along_y[offset] != 0.0:
            weighted = along_y[offset] * partial_x[..., offset : offset + col_count]
            running = weighted if running is None else running + weighted
    return running


def mirrored(padded, along_x, along_y):
    return correlate(padded, along_x[::-1], along_y[::-1])


def strains(padded):
    along_u, along_v, along_w = (padded[0], padded[1], padded[2])
    return jnp.stack(
        [
            correlate(along_u, BASIS_SLOPE, BASIS_VALUE),
            correlate(along_v, BASIS_VALUE, BASIS_SLOPE)
            + HOOP_CURVATURE * correlate(along_w, BASIS_VALUE, BASIS_VALUE),
            correlate(along_u, BASIS_VALUE, BASIS_SLOPE)
            + correlate(along_v, BASIS_SLOPE, BASIS_VALUE),
            -correlate(along_w, BASIS_CURVE, BASIS_VALUE),
            -correlate(along_w, BASIS_VALUE, BASIS_CURVE),
            -2.0 * correlate(along_w, BASIS_SLOPE, BASIS_SLOPE),
        ]
    )


def forces(spread):
    force_u = mirrored(spread[0], BASIS_SLOPE, BASIS_VALUE) + mirrored(
        spread[2], BASIS_VALUE, BASIS_SLOPE
    )
    force_v = mirrored(spread[1], BASIS_VALUE, BASIS_SLOPE) + mirrored(
        spread[2], BASIS_SLOPE, BASIS_VALUE
    )
    force_w = (
        HOOP_CURVATURE * mirrored(spread[1], BASIS_VALUE, BASIS_VALUE)
        - mirrored(spread[3], BASIS_CURVE, BASIS_VALUE)
        - mirrored(spread[4], BASIS_VALUE, BASIS_CURVE)
        - 2.0 * mirrored(spread[5], BASIS_SLOPE, BASIS_SLOPE)
    )
    return jnp.stack([force_u, force_v, force_w])


def apply_layup(stiffness_map, strain):
    running = stiffness_map[:, 0] * strain[0]
    for column in range(1, 6):
        running = running + stiffness_map[:, column] * strain[column]
    return running


def outer_product(left, right):
    return lax.dot_general(
        left, right, (((1,), (1,)), ((), ())), preferred_element_type=jnp.float32
    )


def forward_mlp(inputs, w_first, w_mid, w_last):
    hidden_layer = jnp.tanh(jnp.dot(w_first, inputs, preferred_element_type=jnp.float32)).astype(
        jnp.bfloat16
    )
    activations = [hidden_layer]
    for layer_index in range(w_mid.shape[0]):
        hidden_layer = jnp.tanh(
            jnp.dot(w_mid[layer_index], hidden_layer, preferred_element_type=jnp.float32)
        ).astype(jnp.bfloat16)
        activations.append(hidden_layer)
    return (jnp.dot(w_last, hidden_layer, preferred_element_type=jnp.float32), activations)


def backward_mlp(inputs, activations, upstream, w_mid, w_last):
    grad_last = outer_product(upstream, activations[-1])
    signal = jnp.dot(w_last.T, upstream, preferred_element_type=jnp.float32)
    derivative = (signal * (1.0 - jnp.square(activations[-1].astype(jnp.float32)))).astype(
        jnp.bfloat16
    )
    mid_grads = []
    for layer_index in range(w_mid.shape[0] - 1, -1, -1):
        mid_grads.append(outer_product(derivative, activations[layer_index]))
        signal = jnp.dot(w_mid[layer_index].T, derivative, preferred_element_type=jnp.float32)
        derivative = (
            signal * (1.0 - jnp.square(activations[layer_index].astype(jnp.float32)))
        ).astype(jnp.bfloat16)
    grad_first = outer_product(derivative, inputs)
    return (grad_first, jnp.stack(mid_grads[::-1]), grad_last)


def two_products(remainder, mapped):
    return lax.psum((jnp.sum(remainder * remainder), jnp.sum(remainder * mapped)), ("patch", "sub"))


def per_device(displacement, load, foundation, layup, layup_stiffness, w_first, w_mid, w_last):
    layup_count = layup_stiffness.shape[0]
    onehot = (layup[None] == jnp.arange(layup_count, dtype=jnp.int32)[:, None, None]).astype(
        jnp.float32
    )
    stiffness_map = jnp.einsum(
        "lab,lxy->abxy", layup_stiffness, onehot, precision=lax.Precision.HIGHEST
    )

    def operate(search):
        padded = padded_2(search, (("patch", 1), ("sub", 2)), 1)
        element_stress = apply_layup(stiffness_map, strains(padded))
        spread = padded_2(element_stress, (("patch", 1), ("sub", 2)), 1)
        return forces(spread) + foundation * search

    padded = padded_2(displacement, (("patch", 1), ("sub", 2)), 1)
    strain = strains(padded)
    inputs = strain.reshape(6, -1).astype(jnp.bfloat16)
    learned, activations = forward_mlp(inputs, w_first, w_mid, w_last)
    stress = apply_layup(stiffness_map, strain) + learned.reshape(strain.shape)
    spread = padded_2(stress, (("patch", 1), ("sub", 2)), 1)
    residual = forces(spread) + foundation * displacement - load
    adjoint = jnp.zeros_like(residual)
    remainder = residual
    mapped = operate(remainder)
    norm_now, curved = two_products(remainder, mapped)
    step_size = norm_now / curved
    direction, mapped_dir = (remainder, mapped)
    for step_index in range(ITERS):
        adjoint = adjoint + step_size * direction
        remainder = remainder - step_size * mapped_dir
        if step_index + 1 < ITERS:
            mapped = operate(remainder)
            norm_next, curved = two_products(remainder, mapped)
            beta_ratio = norm_next / norm_now
            step_size = norm_next / (curved - beta_ratio * norm_next / step_size)
            direction = remainder + beta_ratio * direction
            mapped_dir = mapped + beta_ratio * mapped_dir
            norm_now = norm_next
    cycle = padded_2(adjoint, (("patch", 1), ("sub", 2)), 1)
    upstream = strains(cycle).reshape(6, -1).astype(jnp.bfloat16)
    grad_first, grad_mid, grad_last = backward_mlp(inputs, activations, upstream, w_mid, w_last)
    totals = lax.psum((grad_first, grad_mid, grad_last), ("patch", "sub"))
    return (residual, adjoint, totals[0], totals[1], totals[2])


def solution(mesh):
    in_specs = (
        P(None, "patch", "sub"),
        P(None, "patch", "sub"),
        P(None, "patch", "sub"),
        P("patch", "sub"),
        P(),
        P(),
        P(),
        P(),
    )
    out_specs = (P(None, "patch", "sub"), P(None, "patch", "sub"), P(), P(), P())
    return jax.shard_map(
        per_device, mesh=mesh, in_specs=in_specs, out_specs=out_specs, check_vma=False
    )
```

profile of v0, /device:TPU:8, one launch (start us, length us, event | category | flops | bytes accessed | tf_op | source)
XLA Modules:
  0.0 525.6 jit_solution(10310662434873777303)
XLA Ops:
  11.3 2.6 convolution_bitcast_fusion
  20.4 2.5 fusion.3
  59.6 2.3 collective-permute-start.12
  70.7 2.3 concatenate.77
  75.7 44.3 %all-reduce.4 = (f32[]{:T(128)}, f32[]{:T(128)}) all-reduce(f32[]{:T(128)} %get-tuple-element.12, f32[]{:T(128)} %get-tuple-element.11), channel_id=1, replica_groups=mesh['patch'=8,'sub'=4] {'patch','sub'}, use_global_device_ids=true, to_apply=%region_1.0 | all-reduce | flops 2 | bytes 16 | tf_op jit(solution)/shard_map/psum | solution.py:125
  121.4 2.3 collective-permute-start.16
  134.6 2.3 collective-permute-start.20
  146.0 2.3 concatenate.81
  151.1 41.7 %all-reduce.3 = (f32[]{:T(128)}, f32[]{:T(128)}) all-reduce(f32[]{:T(128)} %get-tuple-element.10, f32[]{:T(128)} %get-tuple-element.9), channel_id=1, replica_groups=mesh['patch'=8,'sub'=4] {'patch','sub'}, use_global_device_ids=true, to_apply=%region_5.0 | all-reduce | flops 2 | bytes 16 | tf_op jit(solution)/shard_map/psum | solution.py:125
  198.3 2.3 collective-permute-start.24
  214.1 2.6 collective-permute-start.28
  223.7 2.3 collective-permute-done.30
  226.0 2.3 concatenate.85
  231.6 41.5 %all-reduce.2 = (f32[]{:T(128)}, f32[]{:T(128)}) all-reduce(f32[]{:T(128)} %get-tuple-element.8, f32[]{:T(128)} %get-tuple-element.7), channel_id=1, replica_groups=mesh['patch'=8,'sub'=4] {'patch','sub'}, use_global_device_ids=true, to_apply=%region_9.0 | all-reduce | flops 2 | bytes 16 | tf_op jit(solution)/shard_map/psum | solution.py:125
  278.4 2.3 collective-permute-start.32
  306.3 41.7 %all-reduce.1 = (f32[]{:T(128)}, f32[]{:T(128)}) all-reduce(f32[]{:T(128)} %get-tuple-element.6, f32[]{:T(128)} %get-tuple-element.5), channel_id=1, replica_groups=mesh['patch'=8,'sub'=4] {'patch','sub'}, use_global_device_ids=true, to_apply=%region_13.0 | all-reduce | flops 2 | bytes 16 | tf_op jit(solution)/shard_map/psum | solution.py:125
  352.1 2.3 collective-permute-start.40
  363.9 4.4 fusion.7
  373.2 3.7 fusion.1
  376.9 5.6 %fusion.8 = f32[128,6]{0,1:T(8,128)S(1)} fusion(bf16[6,16384]{1,0:T(8,128)(2,1)S(1)} %copy-done.20, bf16[16384,128]{1,0:T(8,128)(2,1)} %fusion.1, bf16[16384,128]{1,0:T(8,128)(2,1)} %copy-done.5, bf16[3,128,128]{2,1,0:T(8,128)(2,1)S(1)} %copy-done.29), kind=kOutput, calls=%fused_computation.17 | convolution fusion | flops 572522496 | bytes 8686592 | tf_op jit(solution)/shard_map/dot_general | solution.py:89
  382.5 4.8 convolution_bitcast_fusion.3
  388.0 2.8 fusion.390
  390.8 41.5 %all-reduce = (f32[128,6]{0,1:T(8,128)}, f32[6,128]{1,0:T(8,128)}) all-reduce(f32[128,6]{0,1:T(8,128)S(1)} %fusion.8, f32[6,128]{1,0:T(8,128)S(1)} %fusion.390), channel_id=1, replica_groups=mesh['patch'=8,'sub'=4] {'patch','sub'}, use_global_device_ids=true, to_apply=%region_16.0 | all-reduce | flops 1536 | bytes 12288 | tf_op jit(solution)/shard_map/psum | solution.py:170
  432.4 84.5 %all-reduce.7.cloned.1.call-done = f32[3,128,128]{2,1,0:T(8,128)} async-done(((f32[3,128,128]{2,1,0:T(8,128)}), f32[3,128,128]{2,1,0:T(8,128)}) %all-reduce.7.cloned.1.call-update) | async-done | bytes 196624 | tf_op jit(solution)/shard_map/psum | solution.py:170
  (272 shorter events, 148.9 us)
Async XLA Ops:
  7.2 509.7 %all-reduce.7.cloned.1.call-start = ((), (), s32[]{:S(2)}) async-start(), calls=%async_computation | async-start | bytes 393216 | tf_op jit(solution)/shard_map/psum | solution.py:170
  8.3 5.6 %collective-permute-start = (f32[3,1,2048]{2,1,0:T(1,128)S(1)}, f32[3,1,2048]{2,1,0:T(1,128)S(1)}, u32[]{:S(2)}, u32[]{:S(2)}) collective-permute-start(f32[3,1,2048]{2,1,0:T(1,128)S(1)} %get-tuple-element.160), channel_id=1, source_target_pairs={{0,4},{4,8},{8,12},{12,16},{16,20},{20,24},{24,28},{28,0},{1,5},{5... | collective-permute-start | bytes 73736 | tf_op jit(solution)/shard_map/ppermute | solution.py:20
  9.8 4.1 collective-permute-start.1
  33.1 5.0 collective-permute-start.4
  35.3 4.5 collective-permute-start.5
  40.1 3.9 collective-permute-start.6
  47.2 4.8 collective-permute-start.8
  49.0 3.8 collective-permute-start.9
  59.6 5.0 collective-permute-start.12
  61.9 4.1 collective-permute-start.13
  121.4 4.8 collective-permute-start.16
  123.7 3.8 collective-permute-start.17
  134.6 5.1 collective-permute-start.20
  136.8 4.1 collective-permute-start.21
  142.0 4.0 collective-permute-start.22
  198.3 4.8 collective-permute-start.24
  214.1 5.0 collective-permute-start.28
  216.7 4.1 collective-permute-start.29
  221.9 4.1 collective-permute-start.30
  278.4 4.8 collective-permute-start.32
  294.1 5.1 collective-permute-start.36
  296.3 4.1 collective-permute-start.37
  300.7 4.0 collective-permute-start.38
  352.1 4.8 collective-permute-start.40
  (52 other events, 732.7 us)
Sparse Core Ops, SparseCore 0:
  388.1 128.7 all-reduce.6
where the time goes:
time: 535 us; the launch traced here: 526 us
  blocking collectives  211 us (39%)
  waiting for transfers between devices  149 us (28%)
  starting transfers between devices  39 us (7%)
  matrix products  35.5 us (7%)
  local copies, waits for them, and re-layouts  33.1 us (6%)
  between operations  29.3 us (5%)
  other arithmetic  28.6 us (5%)
    psum x4, blocking collectives, two_products(): lax.psum((jnp.sum(remainder * remainder), jnp.sum(remainder * mapped)), (...  169 us
    psum x1, waiting for transfers between devices, per_device(): totals = lax.psum((grad_first, grad_mid, grad_last), ('patch', 'sub'))  84.5 us
    psum x1, blocking collectives, per_device(): totals = lax.psum((grad_first, grad_mid, grad_last), ('patch', 'sub'))  41.5 us
    ppermute x22, waiting for transfers between devices, padded_2(): lax.ppermute(tail, axis, [(i, (i + 1) % count) for i in range(count)])  40.1 us
    ppermute x22, starting transfers between devices, padded_2(): lax.ppermute(tail, axis, [(i, (i + 1) % count) for i in range(count)])  29.5 us
    ppermute x22, waiting for transfers between devices, padded_2(): lax.ppermute(head, axis, [((i + 1) % count, i) for i in range(count)])  24.7 us
    concatenate x11, local copies, waits for them, and re-layouts, padded_2(): jnp.concatenate([lax.ppermute(tail, axis, [(i, (i + 1) % count) for i in...  15.9 us
    dot_general x5, matrix products, outer_product(): lax.dot_general(left, right, (((1,), (1,)), ((), ())), preferred_element_...  15.9 us
  transfers between devices with their start and end apart: 45, of which 42 were waited for; matrix products, arithmetic and copies ran while one was open for 1% of the time, Pallas kernels for 0%

commit v1 on v0

--- a/solution.py
+++ b/solution.py
@@ -167,7 +167,7 @@
     cycle = padded_2(adjoint, (("patch", 1), ("sub", 2)), 1)
     upstream = strains(cycle).reshape(6, -1).astype(jnp.bfloat16)
     grad_first, grad_mid, grad_last = backward_mlp(inputs, activations, upstream, w_mid, w_last)
-    totals = lax.psum((grad_first, grad_mid, grad_last), ("patch", "sub"))
+    totals = lax.psum(lax.psum((grad_first, grad_mid, grad_last), "patch"), "sub")
     return (residual, adjoint, totals[0], totals[1], totals[2])
 
 

time: 535 us -> 505 us (0.944)
  the two profiles are of different devices: /device:TPU:8 before, /device:TPU:0 now
where the time goes in v1:
time: 505 us; the launch traced here: 495 us
  blocking collectives  186 us (37%)
  waiting for transfers between devices  125 us (25%)
  starting transfers between devices  61.2 us (12%)
  local copies, waits for them, and re-layouts  34.3 us (7%)
  matrix products  29.9 us (6%)
  between operations  29.7 us (6%)
  other arithmetic  28.6 us (6%)
    psum x4, blocking collectives, two_products(): lax.psum((jnp.sum(remainder * remainder), jnp.sum(remainder * mapped)), (...  159 us
    psum x1, waiting for transfers between devices, per_device(): lax.psum((grad_first, grad_mid, grad_last), 'patch')  66.2 us
    ppermute x22, waiting for transfers between devices, padded_2(): lax.ppermute(tail, axis, [(i, (i + 1) % count) for i in range(count)])  43.7 us
    ppermute x22, starting transfers between devices, padded_2(): lax.ppermute(head, axis, [((i + 1) % count, i) for i in range(count)])  37.1 us
    ppermute x22, starting transfers between devices, padded_2(): lax.ppermute(tail, axis, [(i, (i + 1) % count) for i in range(count)])  23.7 us
    psum x1, blocking collectives, per_device(): lax.psum((grad_first, grad_mid, grad_last), 'patch')  19.8 us
    concatenate x11, local copies, waits for them, and re-layouts, padded_2(): jnp.concatenate([lax.ppermute(tail, axis, [(i, (i + 1) % count) for i in...  15.9 us
    unnamed x79, local copies, waits for them, and re-layouts  12.6 us
  transfers between devices with their start and end apart: 46, of which 36 were waited for; matrix products, arithmetic and copies ran while one was open for 3% of the time, Pallas kernels for 0%

profile of v1, /device:TPU:0, one launch (start us, length us, event | category | flops | bytes accessed | tf_op | source)
XLA Modules:
  0.0 494.8 jit_solution(3368392117163665084)
XLA Ops:
  8.3 3.0 collective-permute-start
  11.3 3.1 collective-permute-start.1
  14.4 2.6 convolution_bitcast_fusion
  36.8 4.7 collective-permute-start.5
  50.6 5.0 %collective-permute-start.9 = (f32[3,1,2048]{2,1,0:T(1,128)S(1)}, f32[3,1,2048]{2,1,0:T(1,128)S(1)}, u32[]{:S(2)}, u32[]{:S(2)}) collective-permute-start(f32[3,1,2048]{2,1,0:T(1,128)S(1)} %get-tuple-element.161), channel_id=1, source_target_pairs={{4,0},{8,4},{12,8},{16,12},{20,16},{24,20},{28,24},{0,28},{5,1},{9... | collective-permute-start | bytes 73736 | tf_op jit(solution)/shard_map/ppermute | solution.py:22
  64.1 4.8 collective-permute-start.13
  80.7 39.9 %all-reduce.3 = (f32[]{:T(128)}, f32[]{:T(128)}) all-reduce(f32[]{:T(128)} %get-tuple-element.12, f32[]{:T(128)} %get-tuple-element.11), channel_id=1, replica_groups=mesh['patch'=8,'sub'=4] {'patch','sub'}, use_global_device_ids=true, to_apply=%region_1.0 | all-reduce | flops 2 | bytes 16 | tf_op jit(solution)/shard_map/psum | solution.py:125
  130.2 2.7 collective-permute-done.18
  138.2 2.9 collective-permute-start.21
  153.5 39.8 %all-reduce.2 = (f32[]{:T(128)}, f32[]{:T(128)}) all-reduce(f32[]{:T(128)} %get-tuple-element.10, f32[]{:T(128)} %get-tuple-element.9), channel_id=1, replica_groups=mesh['patch'=8,'sub'=4] {'patch','sub'}, use_global_device_ids=true, to_apply=%region_5.0 | all-reduce | flops 2 | bytes 16 | tf_op jit(solution)/shard_map/psum | solution.py:125
  207.9 3.1 collective-permute-done.26
  218.1 3.0 collective-permute-start.29
  233.9 39.8 %all-reduce.1 = (f32[]{:T(128)}, f32[]{:T(128)}) all-reduce(f32[]{:T(128)} %get-tuple-element.8, f32[]{:T(128)} %get-tuple-element.7), channel_id=1, replica_groups=mesh['patch'=8,'sub'=4] {'patch','sub'}, use_global_device_ids=true, to_apply=%region_9.0 | all-reduce | flops 2 | bytes 16 | tf_op jit(solution)/shard_map/psum | solution.py:125
  288.0 2.6 collective-permute-done.34
  297.7 3.0 collective-permute-start.37
  308.7 39.8 %all-reduce = (f32[]{:T(128)}, f32[]{:T(128)}) all-reduce(f32[]{:T(128)} %get-tuple-element.6, f32[]{:T(128)} %get-tuple-element.5), channel_id=1, replica_groups=mesh['patch'=8,'sub'=4] {'patch','sub'}, use_global_device_ids=true, to_apply=%region_13.0 | all-reduce | flops 2 | bytes 16 | tf_op jit(solution)/shard_map/psum | solution.py:125
  361.0 3.0 collective-permute-done.42
  365.9 4.4 fusion.7
  380.5 5.6 %fusion.8 = f32[128,6]{0,1:T(8,128)S(1)} fusion(bf16[6,16384]{1,0:T(8,128)(2,1)S(1)} %copy-done.22, bf16[16384,128]{1,0:T(8,128)(2,1)} %copy-done.8, bf16[16384,128]{1,0:T(8,128)(2,1)} %copy-done.5, bf16[3,128,128]{2,1,0:T(8,128)(2,1)S(1)} %copy-done.31), kind=kOutput, calls=%fused_computation.17 | convolution fusion | flops 572522496 | bytes 8686592 | tf_op jit(solution)/shard_map/dot_general | solution.py:89
  386.1 66.2 %all-reduce.9.cloned.1.call-done = f32[3,128,128]{2,1,0:T(8,128)} async-done(((f32[3,128,128]{2,1,0:T(8,128)}), f32[3,128,128]{2,1,0:T(8,128)}) %all-reduce.9.cloned.1.call-update) | async-done | bytes 196624 | tf_op jit(solution)/shard_map/psum | solution.py:170
  452.4 2.8 fusion.390
  455.2 19.8 %all-reduce.4 = (f32[128,6]{0,1:T(8,128)S(1)}, f32[6,128]{1,0:T(8,128)S(1)}) all-reduce(f32[128,6]{0,1:T(8,128)S(1)} %fusion.8, f32[6,128]{1,0:T(8,128)S(1)} %fusion.390), channel_id=1, replica_groups=mesh['patch'=8,'sub'=4] {'patch'}, use_global_device_ids=true, to_apply=%region_16.0 | all-reduce | flops 1536 | bytes 12288 | tf_op jit(solution)/shard_map/psum | solution.py:170
  475.0 6.5 %all-reduce.5 = (f32[128,6]{0,1:T(8,128)}, f32[6,128]{1,0:T(8,128)}) all-reduce(f32[128,6]{0,1:T(8,128)S(1)} %get-tuple-element.21, f32[6,128]{1,0:T(8,128)S(1)} %get-tuple-element.22), channel_id=1, replica_groups=mesh['patch'=8,'sub'=4] {'sub'}, use_global_device_ids=true, to_apply=%region_17.0 | all-reduce | flops 1536 | bytes 12288 | tf_op jit(solution)/shard_map/psum | solution.py:170
  481.5 4.3 all-reduce.11.cloned.1.call-done
  (280 shorter events, 152.4 us)
Async XLA Ops:
  7.2 445.2 %all-reduce.9.cloned.1.call-start = ((), (), s32[]{:S(2)}) async-start(), calls=%async_computation | async-start | bytes 393216 | tf_op jit(solution)/shard_map/psum | solution.py:170
  8.3 8.7 %collective-permute-start = (f32[3,1,2048]{2,1,0:T(1,128)S(1)}, f32[3,1,2048]{2,1,0:T(1,128)S(1)}, u32[]{:S(2)}, u32[]{:S(2)}) collective-permute-start(f32[3,1,2048]{2,1,0:T(1,128)S(1)} %get-tuple-element.162), channel_id=1, source_target_pairs={{0,4},{4,8},{8,12},{12,16},{16,20},{20,24},{24,28},{28,0},{1,5},{5... | collective-permute-start | bytes 73736 | tf_op jit(solution)/shard_map/ppermute | solution.py:20
  11.3 5.7 %collective-permute-start.1 = (f32[3,1,2048]{2,1,0:T(1,128)S(1)}, f32[3,1,2048]{2,1,0:T(1,128)S(1)}, u32[]{:S(2)}, u32[]{:S(2)}) collective-permute-start(f32[3,1,2048]{2,1,0:T(1,128)S(1)} %get-tuple-element.163), channel_id=1, source_target_pairs={{4,0},{8,4},{12,8},{16,12},{20,16},{24,20},{28,24},{0,28},{5,1},{9... | collective-permute-start | bytes 73736 | tf_op jit(solution)/shard_map/ppermute | solution.py:22
  36.6 6.8 %collective-permute-start.4 = (f32[6,1,2048]{2,1,0:T(1,128)S(1)}, f32[6,1,2048]{2,1,0:T(1,128)S(1)}, u32[]{:S(2)}, u32[]{:S(2)}) collective-permute-start(f32[6,1,2048]{2,1,0:T(1,128)S(1)} %get-tuple-element.148), channel_id=1, source_target_pairs={{0,4},{4,8},{8,12},{12,16},{16,20},{20,24},{24,28},{28,0},{1,5},{5... | collective-permute-start | bytes 147464 | tf_op jit(solution)/shard_map/ppermute | solution.py:20
  36.8 6.6 %collective-permute-start.5 = (f32[6,1,2048]{2,1,0:T(1,128)S(1)}, f32[6,1,2048]{2,1,0:T(1,128)S(1)}, u32[]{:S(2)}, u32[]{:S(2)}) collective-permute-start(f32[6,1,2048]{2,1,0:T(1,128)S(1)} %get-tuple-element.149), channel_id=1, source_target_pairs={{4,0},{8,4},{12,8},{16,12},{20,16},{24,20},{28,24},{0,28},{5,1},{9... | collective-permute-start | bytes 147464 | tf_op jit(solution)/shard_map/ppermute | solution.py:22
  50.5 6.8 %collective-permute-start.8 = (f32[3,1,2048]{2,1,0:T(1,128)S(1)}, f32[3,1,2048]{2,1,0:T(1,128)S(1)}, u32[]{:S(2)}, u32[]{:S(2)}) collective-permute-start(f32[3,1,2048]{2,1,0:T(1,128)S(1)} %get-tuple-element.160), channel_id=1, source_target_pairs={{0,4},{4,8},{8,12},{12,16},{16,20},{20,24},{24,28},{28,0},{1,5},{5... | collective-permute-start | bytes 73736 | tf_op jit(solution)/shard_map/ppermute | solution.py:20
  50.6 6.7 %collective-permute-start.9 = (f32[3,1,2048]{2,1,0:T(1,128)S(1)}, f32[3,1,2048]{2,1,0:T(1,128)S(1)}, u32[]{:S(2)}, u32[]{:S(2)}) collective-permute-start(f32[3,1,2048]{2,1,0:T(1,128)S(1)} %get-tuple-element.161), channel_id=1, source_target_pairs={{4,0},{8,4},{12,8},{16,12},{20,16},{24,20},{28,24},{0,28},{5,1},{9... | collective-permute-start | bytes 73736 | tf_op jit(solution)/shard_map/ppermute | solution.py:22
  64.1 6.9 %collective-permute-start.12 = (f32[6,1,2048]{2,1,0:T(1,128)S(1)}, f32[6,1,2048]{2,1,0:T(1,128)S(1)}, u32[]{:S(2)}, u32[]{:S(2)}) collective-permute-start(f32[6,1,2048]{2,1,0:T(1,128)S(1)} %get-tuple-element.144), channel_id=1, source_target_pairs={{0,4},{4,8},{8,12},{12,16},{16,20},{20,24},{24,28},{28,0},{1,5},{5... | collective-permute-start | bytes 147464 | tf_op jit(solution)/shard_map/ppermute | solution.py:20
  64.1 6.8 %collective-permute-start.13 = (f32[6,1,2048]{2,1,0:T(1,128)S(1)}, f32[6,1,2048]{2,1,0:T(1,128)S(1)}, u32[]{:S(2)}, u32[]{:S(2)}) collective-permute-start(f32[6,1,2048]{2,1,0:T(1,128)S(1)} %get-tuple-element.145), channel_id=1, source_target_pairs={{4,0},{8,4},{12,8},{16,12},{20,16},{24,20},{28,24},{0,28},{5,1},{9... | collective-permute-start | bytes 147464 | tf_op jit(solution)/shard_map/ppermute | solution.py:22
  122.0 6.6 %collective-permute-start.16 = (f32[3,1,2048]{2,1,0:T(1,128)S(1)}, f32[3,1,2048]{2,1,0:T(1,128)S(1)}, u32[]{:S(2)}, u32[]{:S(2)}) collective-permute-start(f32[3,1,2048]{2,1,0:T(1,128)S(1)} %get-tuple-element.158), channel_id=1, source_target_pairs={{0,4},{4,8},{8,12},{12,16},{16,20},{20,24},{24,28},{28,0},{1,5},{5... | collective-permute-start | bytes 73736 | tf_op jit(solution)/shard_map/ppermute | solution.py:20
  124.3 4.3 collective-permute-start.17
  128.7 4.3 collective-permute-start.18
  136.3 6.9 %collective-permute-start.20 = (f32[6,1,2048]{2,1,0:T(1,128)S(1)}, f32[6,1,2048]{2,1,0:T(1,128)S(1)}, u32[]{:S(2)}, u32[]{:S(2)}) collective-permute-start(f32[6,1,2048]{2,1,0:T(1,128)S(1)} %get-tuple-element.140), channel_id=1, source_target_pairs={{0,4},{4,8},{8,12},{12,16},{16,20},{20,24},{24,28},{28,0},{1,5},{5... | collective-permute-start | bytes 147464 | tf_op jit(solution)/shard_map/ppermute | solution.py:20
  138.2 5.1 %collective-permute-start.21 = (f32[6,1,2048]{2,1,0:T(1,128)S(1)}, f32[6,1,2048]{2,1,0:T(1,128)S(1)}, u32[]{:S(2)}, u32[]{:S(2)}) collective-permute-start(f32[6,1,2048]{2,1,0:T(1,128)S(1)} %get-tuple-element.141), channel_id=1, source_target_pairs={{4,0},{8,4},{12,8},{16,12},{20,16},{24,20},{28,24},{0,28},{5,1},{9... | collective-permute-start | bytes 147464 | tf_op jit(solution)/shard_map/ppermute | solution.py:22
  198.9 6.6 %collective-permute-start.24 = (f32[3,1,2048]{2,1,0:T(1,128)S(1)}, f32[3,1,2048]{2,1,0:T(1,128)S(1)}, u32[]{:S(2)}, u32[]{:S(2)}) collective-permute-start(f32[3,1,2048]{2,1,0:T(1,128)S(1)} %get-tuple-element.156), channel_id=1, source_target_pairs={{0,4},{4,8},{8,12},{12,16},{16,20},{20,24},{24,28},{28,0},{1,5},{5... | collective-permute-start | bytes 73736 | tf_op jit(solution)/shard_map/ppermute | solution.py:20
  206.4 4.6 collective-permute-start.26
  216.3 6.9 %collective-permute-start.28 = (f32[6,1,2048]{2,1,0:T(1,128)S(1)}, f32[6,1,2048]{2,1,0:T(1,128)S(1)}, u32[]{:S(2)}, u32[]{:S(2)}) collective-permute-start(f32[6,1,2048]{2,1,0:T(1,128)S(1)} %get-tuple-element.136), channel_id=1, source_target_pairs={{0,4},{4,8},{8,12},{12,16},{16,20},{20,24},{24,28},{28,0},{1,5},{5... | collective-permute-start | bytes 147464 | tf_op jit(solution)/shard_map/ppermute | solution.py:20
  218.1 5.1 %collective-permute-start.29 = (f32[6,1,2048]{2,1,0:T(1,128)S(1)}, f32[6,1,2048]{2,1,0:T(1,128)S(1)}, u32[]{:S(2)}, u32[]{:S(2)}) collective-permute-start(f32[6,1,2048]{2,1,0:T(1,128)S(1)} %get-tuple-element.137), channel_id=1, source_target_pairs={{4,0},{8,4},{12,8},{16,12},{20,16},{24,20},{28,24},{0,28},{5,1},{9... | collective-permute-start | bytes 147464 | tf_op jit(solution)/shard_map/ppermute | solution.py:22
  279.0 6.6 %collective-permute-start.32 = (f32[3,1,2048]{2,1,0:T(1,128)S(1)}, f32[3,1,2048]{2,1,0:T(1,128)S(1)}, u32[]{:S(2)}, u32[]{:S(2)}) collective-permute-start(f32[3,1,2048]{2,1,0:T(1,128)S(1)} %get-tuple-element.154), channel_id=1, source_target_pairs={{0,4},{4,8},{8,12},{12,16},{16,20},{20,24},{24,28},{28,0},{1,5},{5... | collective-permute-start | bytes 73736 | tf_op jit(solution)/shard_map/ppermute | solution.py:20
  295.9 6.9 %collective-permute-start.36 = (f32[6,1,2048]{2,1,0:T(1,128)S(1)}, f32[6,1,2048]{2,1,0:T(1,128)S(1)}, u32[]{:S(2)}, u32[]{:S(2)}) collective-permute-start(f32[6,1,2048]{2,1,0:T(1,128)S(1)} %get-tuple-element.132), channel_id=1, source_target_pairs={{0,4},{4,8},{8,12},{12,16},{16,20},{20,24},{24,28},{28,0},{1,5},{5... | collective-permute-start | bytes 147464 | tf_op jit(solution)/shard_map/ppermute | solution.py:20
  297.7 5.1 %collective-permute-start.37 = (f32[6,1,2048]{2,1,0:T(1,128)S(1)}, f32[6,1,2048]{2,1,0:T(1,128)S(1)}, u32[]{:S(2)}, u32[]{:S(2)}) collective-permute-start(f32[6,1,2048]{2,1,0:T(1,128)S(1)} %get-tuple-element.133), channel_id=1, source_target_pairs={{4,0},{8,4},{12,8},{16,12},{20,16},{24,20},{28,24},{0,28},{5,1},{9... | collective-permute-start | bytes 147464 | tf_op jit(solution)/shard_map/ppermute | solution.py:22
  352.7 6.6 %collective-permute-start.40 = (f32[3,1,2048]{2,1,0:T(1,128)S(1)}, f32[3,1,2048]{2,1,0:T(1,128)S(1)}, u32[]{:S(2)}, u32[]{:S(2)}) collective-permute-start(f32[3,1,2048]{2,1,0:T(1,128)S(1)} %get-tuple-element.152), channel_id=1, source_target_pairs={{0,4},{4,8},{8,12},{12,16},{16,20},{20,24},{24,28},{28,0},{1,5},{5... | collective-permute-start | bytes 73736 | tf_op jit(solution)/shard_map/ppermute | solution.py:20
  359.4 4.5 collective-permute-start.42
  380.1 105.7 %all-reduce.11.cloned.1.call-start = ((), (), s32[]{:S(2)}) async-start(), calls=%async_computation.1 | async-start | bytes 393216 | tf_op jit(solution)/shard_map/psum | solution.py:170
  (55 other events, 737.9 us)
Sparse Core Ops, SparseCore 0:
  380.2 72.0 all-reduce.8
  454.7 31.1 all-reduce.10
